TPU v7x, 512 devices: a whole 4x8x8 slice. The times are simulated.
512 devices in a mesh: ctx: 16 (over x, z_hi), row: 8 (over y), batch: 4 (over z_lo, core).
Axes of the slice: x: 4, y: 8, z: 8 (z_hi: 4, z_lo: 2; z = z_hi * 2 + z_lo), core: 2. Of those that a mesh axis runs over, the one named last changes fastest.
Arguments:
- queries: bfloat16 [12288, 5120], P(('batch', 'ctx'), 'row'), parts along dimension 0
- keys: bfloat16 [12288, 5120], P(('batch', 'ctx'), 'row'), parts along dimension 0
- values: bfloat16 [12288, 5120], P(('batch', 'ctx'), 'row'), parts along dimension 0, may hold values from -6 to 6
- gain_q: float32 [5120], P('row'), may hold values from 1.2 to 2.4
- gain_k: float32 [5120], P('row'), may hold values from 1.2 to 2.4
- clip_ids: int32 [12288], P(('batch', 'ctx')), parts along dimension 0, may hold values from 0 to 3, never falling along the last dimension, each value on 1 to 1920 neighbouring positions
- clip_grid: int32 [16, 2], P('batch'), parts along dimension 0, may hold values from 8 to 40
Outputs:
- attended: bfloat16 [12288, 5120], P(('batch', 'ctx'), 'row'), parts along dimension 0
There are 4 independent parts, one for each index of `batch`. A program takes and returns all parts, laid end to end along the dimension named above; an argument that names none is the same for every part. Nothing has to cross between parts.
Inputs may be any that keep to these rules, and one draw needn't show every extreme that they name: `clip_ids`: never falls along the tokens; each of the 4 clips has 1 to 1920 tokens, and one has exactly 1920.
All inputs are finite; a program needn't handle non-finite values.
Results may differ from a plain program's by a relative error of at most 0.012.
The roundings to bfloat16 on the way count: a program that leaves them out, or rounds other values in their place, can miss the bound.
Values may be sent and summed in bfloat16 or wider, within the bound.
A program may use at most 64 MiB of HBM per device.

v0:
```python
import math
import jax
import jax.numpy as jnp
from jax import lax
from jax.sharding import PartitionSpec as P

HD = 128
D = 5120
CLIPS = 4
EPSILON = 1e-06
NEGATIVE = -1e30
ROTARY_BASE = 10000.0
block_limit = 1024


def lookup(lookup_table, positions):
    labels = jnp.arange(lookup_table.shape[0], dtype=jnp.int32)
    return jnp.sum(
        jnp.where(positions[:, None] == labels[None, :], lookup_table[None, :], 0), axis=1
    )


def spin(matrix, offsets, clip_of, clip_grid, head_size):
    row_count = matrix.shape[0]
    sixth_part = head_size // 6
    first_dims = head_size - 4 * sixth_part
    first_freqs = 1.0 / ROTARY_BASE ** (
        jnp.arange(0, first_dims, 2, dtype=jnp.float32) / first_dims
    )
    other_freqs = 1.0 / ROTARY_BASE ** (
        jnp.arange(0, 2 * sixth_part, 2, dtype=jnp.float32) / (2 * sixth_part)
    )
    heights = lookup(clip_grid[:, 0], clip_of)
    widths = lookup(clip_grid[:, 1], clip_of)
    frame_pos = offsets // (heights * widths)
    line_pos = offsets // widths % heights
    column_pos = offsets % widths
    angles = jnp.concatenate(
        [
            frame_pos.astype(jnp.float32)[:, None] * first_freqs[None, :],
            line_pos.astype(jnp.float32)[:, None] * other_freqs[None, :],
            column_pos.astype(jnp.float32)[:, None] * other_freqs[None, :],
        ],
        axis=1,
    )
    cosine = jnp.repeat(jnp.cos(angles), 2, axis=1)
    sine_table = jnp.repeat(jnp.sin(angles), 2, axis=1)
    feature = jnp.arange(head_size, dtype=jnp.int32)
    is_even = (feature % 2 == 0)[None, None, :]
    head_view = matrix.reshape(row_count, -1, head_size)
    partner = jnp.where(is_even, -jnp.roll(head_view, -1, axis=2), jnp.roll(head_view, 1, axis=2))
    turned = head_view * cosine[:, None, :] + partner * sine_table[:, None, :]
    return turned.reshape(row_count, -1)


def on_device(queries, keys, values, gain_q, gain_k, clip_ids, clip_grid):
    rows_here, width_here = queries.shape
    heads_here = width_here // HD
    score_scale = 1.0 / math.sqrt(HD)
    query_wide = queries.astype(jnp.float32)
    key_wide = keys.astype(jnp.float32)
    squares = lax.psum(
        (jnp.sum(query_wide * query_wide, axis=1), jnp.sum(key_wide * key_wide, axis=1)), "row"
    )
    query_scale = lax.rsqrt(squares[0] / D + EPSILON)
    key_scale = lax.rsqrt(squares[1] / D + EPSILON)
    labels = jnp.arange(CLIPS, dtype=jnp.int32)
    local_counts = jnp.sum((clip_ids[:, None] == labels[None, :]).astype(jnp.int32), axis=0)
    totals = lax.psum(local_counts, "ctx")
    starts = jnp.cumsum(totals) - totals
    first_row = lax.axis_index("ctx") * rows_here
    offsets = first_row + jnp.arange(rows_here, dtype=jnp.int32) - lookup(starts, clip_ids)
    query_rot = spin(
        query_wide * query_scale[:, None] * gain_q[None, :], offsets, clip_ids, clip_grid, HD
    ).astype(jnp.bfloat16)
    query_heads = query_rot.reshape(rows_here, heads_here, HD)
    key_send = spin(
        key_wide * key_scale[:, None] * gain_k[None, :], offsets, clip_ids, clip_grid, HD
    ).astype(jnp.bfloat16)
    initial = (
        jnp.full((heads_here, rows_here), NEGATIVE, jnp.float32),
        jnp.zeros((heads_here, rows_here), jnp.float32),
        jnp.zeros((rows_here, heads_here, HD), jnp.float32),
    )
    running = initial
    piece_start = jnp.int32(0)
    key_piece = lax.all_gather(key_send, "ctx", axis=0, tiled=True)
    value_piece = lax.all_gather(values, "ctx", axis=0, tiled=True)
    row_count = key_piece.shape[0]
    block_rows = min(row_count, block_limit)
    for block_first in range(0, row_count, block_rows):
        block_size = min(block_rows, row_count - block_first)
        fold_key_rows = key_piece[block_first : block_first + block_size]
        fold_value_rows = value_piece[block_first : block_first + block_size]
        key_index = piece_start + block_first + jnp.arange(fold_key_rows.shape[0], dtype=jnp.int32)
        key_key_clips = (
            jnp.sum((starts[None, :] <= key_index[:, None]).astype(jnp.int32), axis=1) - 1
        )
        peak_old, total_old, summed_old = running
        key_view = fold_key_rows.reshape(fold_key_rows.shape[0], heads_here, HD)
        value_view = fold_value_rows.reshape(fold_value_rows.shape[0], heads_here, HD)
        scores = (
            jnp.einsum("qhd,khd->hqk", query_heads, key_view, preferred_element_type=jnp.float32)
            * score_scale
        )
        same = clip_ids[:, None] == key_key_clips[None, :]
        masked = jnp.where(same[None, :, :], scores, NEGATIVE)
        peak_new = jnp.maximum(peak_old, jnp.max(masked, axis=2))
        weights = jnp.where(same[None, :, :], jnp.exp(masked - peak_new[:, :, None]), 0.0)
        factor = jnp.exp(peak_old - peak_new)
        total_new = total_old * factor + jnp.sum(weights, axis=2)
        summed = summed_old * jnp.transpose(factor)[:, :, None] + jnp.einsum(
            "hqk,khd->qhd",
            weights.astype(jnp.bfloat16),
            value_view,
            preferred_element_type=jnp.float32,
        )
        running = (peak_new, total_new, summed)
    attended = running[2] / jnp.transpose(running[1])[:, :, None]
    return attended.reshape(rows_here, width_here).astype(jnp.bfloat16)


def solution(mesh):
    in_specs = (
        P(("batch", "ctx"), "row"),
        P(("batch", "ctx"), "row"),
        P(("batch", "ctx"), "row"),
        P("row"),
        P("row"),
        P(("batch", "ctx")),
        P("batch", None),
    )
    out_specs = P(("batch", "ctx"), "row")
    return jax.shard_map(
        on_device, mesh=mesh, in_specs=in_specs, out_specs=out_specs, check_vma=False
    )
```

profile of v0, /device:TPU:1, one launch (start us, length us, event | category | flops | bytes accessed | tf_op | source)
XLA Modules:
  0.0 213.5 jit_solution(10910715953771418640)
XLA Ops:
  8.1 20.5 %psum.21 = s32[4]{0:T(128)S(1)} all-reduce(s32[4]{0:T(128)S(1)} %convert_reduce_fusion.3), channel_id=1, replica_groups=mesh['ctx'=16,'row'=8,'batch'=4] {'ctx'}, use_global_device_ids=true, to_apply=%region_1.0 | all-reduce | flops 4 | bytes 32 | tf_op jit(solution)/shard_map/psum | solution.py:69
  31.3 1.1 copy.45
  32.5 1.1 copy.46
  33.8 15.1 %all-reduce = (f32[192]{0:T(256)S(1)}, f32[192]{0:T(256)S(1)}) all-reduce(f32[192]{0:T(256)S(1)} %fusion.48, f32[192]{0:T(256)S(1)} %fusion.50), channel_id=1, replica_groups=mesh['ctx'=16,'row'=8,'batch'=4] {'row'}, use_global_device_ids=true, to_apply=%region_5.0 | all-reduce | flops 384 | bytes 3072 | tf_op jit(solution)/shard_map/psum | solution.py:62
  51.2 0.9 copy.47
  52.6 44.7 %all-gather.5.cloned.1.call-done = bf16[3072,640]{1,0:T(8,128)(2,1)} async-done(((bf16[192,640]{1,0:T(8,128)(2,1)}), bf16[3072,640]{1,0:T(8,128)(2,1)}) %all-gather.5.cloned.1.call-update) | async-done | bytes 3932176 | tf_op jit(solution)/shard_map/all_gather | solution.py:88
  97.3 4.0 %fusion.81 = (bf16[1024,640]{1,0:T(8,128)(2,1)S(1)}, bf16[1024,640]{1,0:T(8,128)(2,1)}, bf16[1024,640]{1,0:T(8,128)(2,1)}) fusion(bf16[3072,640]{1,0:T(8,128)(2,1)} %all-gather.5.cloned.1.call-done), kind=kLoop, calls=%fused_computation.121 | loop fusion | bytes 7864320 | tf_op jit(solution)/shard_map/slice | solution.py:94
  101.3 1.5 copy.79
  102.8 76.7 %all-gather.3.cloned.1.call-done = bf16[3072,640]{1,0:T(8,128)(2,1)} async-done(((bf16[192,640]{1,0:T(8,128)(2,1)}), bf16[3072,640]{1,0:T(8,128)(2,1)}) %all-gather.3.cloned.1.call-update) | async-done | bytes 3932176 | tf_op jit(solution)/shard_map/all_gather | solution.py:87
  179.5 3.9 %fusion.82 = (bf16[1024,640]{1,0:T(8,128)(2,1)S(1)}, bf16[1024,640]{1,0:T(8,128)(2,1)}, bf16[1024,640]{1,0:T(8,128)(2,1)}) fusion(bf16[3072,640]{1,0:T(8,128)(2,1)} %all-gather.3.cloned.1.call-done), kind=kLoop, calls=%fused_computation.122 | loop fusion | bytes 7864320 | tf_op jit(solution)/shard_map/slice | solution.py:93
  184.1 1.6 copy.76
  185.7 2.5 %copy.74 = bf16[1024,640]{0,1:T(8,128)(2,1)} copy(bf16[1024,640]{1,0:T(8,128)(2,1)} %get-tuple-element.22) | data formatting | bytes 2621440
  188.2 2.5 %copy.77 = bf16[1024,640]{0,1:T(8,128)(2,1)} copy(bf16[1024,640]{1,0:T(8,128)(2,1)} %get-tuple-element.18) | data formatting | bytes 2621440
  190.7 2.5 %copy.75 = bf16[1024,640]{0,1:T(8,128)(2,1)} copy(bf16[1024,640]{1,0:T(8,128)(2,1)} %get-tuple-element.19) | data formatting | bytes 2621440
  193.2 2.4 %fusion = (f32[5,192]{1,0:T(8,128)S(1)}, f32[5,192,1024]{2,1,0:T(8,128)S(1)}) fusion(pred[192,1024]{1,0:T(8,128)(4,1)S(1)} %get-tuple-element.43, bf16[192,5,128]{0,2,1:T(8,128)(2,1)S(1)} %bitcast.131, bf16[1024,5,128]{0,2,1:T(8,128)(2,1)} %bitcast.136), kind=kOutput, calls=%fused_computation.6 | convolution fusion | flops 254606400 | bytes 5689088 | tf_op jit(solution)/shard_map/qhd,khd->hqk/dot_general | solution.py:103
  195.6 1.1 fusion.1
  196.6 1.1 fusion.2
  197.7 1.3 fusion.7
  199.0 1.3 fusion.5
  200.3 1.3 fusion.3
  201.6 1.3 fusion.39
  202.9 1.3 fusion.33
  204.3 1.3 fusion.45
  205.8 0.9 copy.64
  (57 shorter events, 7.9 us)
Async XLA Ops:
  6.5 90.7 %all-gather.5.cloned.1.call-start = ((), (), s32[]{:S(2)}) async-start(), calls=%async_computation.1 | async-start | bytes 4177920 | tf_op jit(solution)/shard_map/all_gather | solution.py:88
  7.3 172.2 %all-gather.3.cloned.1.call-start = ((), (), s32[]{:S(2)}) async-start(), calls=%async_computation | async-start | bytes 4177920 | tf_op jit(solution)/shard_map/all_gather | solution.py:87
  31.3 18.8 %copy-start.3 = (f32[640]{0:T(1024)S(1)}, f32[640]{0:T(1024)}, u32[]{:S(2)}) copy-start(f32[640]{0:T(1024)} %param.11) | copy-start | bytes 7684
  50.0 0.7 copy-start.4
  50.4 1.8 copy-start.5
  199.0 2.6 %copy-start.2 = (bf16[1024,640]{0,1:T(8,128)(2,1)S(1)}, bf16[1024,640]{0,1:T(8,128)(2,1)}, u32[]{:S(2)}) copy-start(bf16[1024,640]{0,1:T(8,128)(2,1)} %copy.75) | copy-start | bytes 3932164
  201.6 1.3 copy-start.1
  202.9 1.3 copy-start
Sparse Core Ops, SparseCore 0:
  10.4 86.8 all-gather.4
  100.3 79.1 all-gather.2
where the time goes:
time: 214 us
  waiting for transfers between devices  122 us (57%)
  blocking collectives  35.7 us (17%)
  local copies, waits for them, and re-layouts  24.8 us (12%)
  between operations  13.8 us (6%)
  other arithmetic  8.73 us (4%)
  matrix products  8.44 us (4%)
    all_gather x1, waiting for transfers between devices, on_device(): key_piece = lax.all_gather(key_send, 'ctx', axis=0, tiled=True)  76.7 us
    all_gather x1, waiting for transfers between devices, on_device(): value_piece = lax.all_gather(values, 'ctx', axis=0, tiled=True)  44.7 us
    psum x1, blocking collectives, on_device(): totals = lax.psum(local_counts, 'ctx')  20.5 us
    psum x1, blocking collectives, on_device(): lax.psum((jnp.sum(query_wide * query_wide, axis=1), jnp.sum(key_wide * ke...  15.1 us
    unnamed x20, local copies, waits for them, and re-layouts  13.6 us
    dot_general x3, matrix products, on_device(): jnp.einsum('qhd,khd->hqk', query_heads, key_view, preferred_element_type=...  4.46 us
  transfers between devices with their start and end apart: 2, of which 2 were waited for; matrix products, arithmetic and copies ran while one was open for 7% of the time, Pallas kernels for 0%

commit v1 on v0

--- a/solution.py
+++ b/solution.py
@@ -85,7 +85,9 @@
     running = initial
     piece_start = jnp.int32(0)
     key_piece = lax.all_gather(key_send, "ctx", axis=0, tiled=True)
-    value_piece = lax.all_gather(values, "ctx", axis=0, tiled=True)
+    value_piece = jnp.concatenate(
+        lax.all_to_all(jnp.stack([values] * lax.axis_size("ctx")), "ctx", 0, 0), axis=0
+    )
     row_count = key_piece.shape[0]
     block_rows = min(row_count, block_limit)
     for block_first in range(0, row_count, block_rows):

time: 214 us -> 244 us (1.14)
  blocking collectives: 35.7 us -> 90.1 us
  waiting for transfers between devices: 122 us -> 81.3 us
  starting transfers between devices: 0.04 us -> 13.6 us
  other arithmetic: 8.73 us -> 11.7 us
    psum x1, blocking collectives: 20.5 us -> 74.6 us  [on_device(): totals = lax.psum(local_counts, 'ctx')]
    all_gather x1 -> x0, waiting for transfers between devices: 44.7 us -> none  [on_device(): value_piece = lax.all_gather(values, 'ctx', axis=0, tiled=True)]
    all_to_all x0 -> x1, starting transfers between devices: none -> 13.6 us  [on_device(): lax.all_to_all(jnp.stack([values] * lax.axis_size('ctx')), 'ctx', 0, 0)]
    unnamed x20 -> x25, local copies, waits for them, and re-layouts: 13.6 us -> 4.21 us
    slice x1 -> x4, local copies, waits for them, and re-layouts: 4.03 us -> 10.5 us  [on_device(): fold_value_rows = value_piece[block_first:block_first + block_size]]
    all_gather x1, waiting for transfers between devices: 76.7 us -> 81.2 us  [on_device(): key_piece = lax.all_gather(key_send, 'ctx', axis=0, tiled=True)]
    another operation x0 -> x1, local copies, waits for them, and re-layouts: none -> 3.3 us  [on_device(): jnp.stack([values] * lax.axis_size('ctx'))]
    concatenate x2, other arithmetic: 0.14 us -> 2.98 us  [spin(): jnp.roll(head_view, 1, axis=2)]
  transfers between devices with their start and end apart: 2 -> 2, of which waited for: 2 -> 1; matrix products, arithmetic and copies ran while one was open for 7% -> 7% of each run, Pallas kernels for 0% -> 0%
where the time goes in v1:
time: 244 us
  blocking collectives  90.1 us (37%)
  waiting for transfers between devices  81.3 us (33%)
  local copies, waits for them, and re-layouts  24.8 us (10%)
  between operations  13.8 us (6%)
  starting transfers between devices  13.6 us (6%)
  other arithmetic  11.7 us (5%)
  matrix products  8.4 us (3%)
    all_gather x1, waiting for transfers between devices, on_device(): key_piece = lax.all_gather(key_send, 'ctx', axis=0, tiled=True)  81.2 us
    psum x1, blocking collectives, on_device(): totals = lax.psum(local_counts, 'ctx')  74.6 us
    psum x1, blocking collectives, on_device(): lax.psum((jnp.sum(query_wide * query_wide, axis=1), jnp.sum(key_wide * ke...  15.5 us
    all_to_all x1, starting transfers between devices, on_device(): lax.all_to_all(jnp.stack([values] * lax.axis_size('ctx')), 'ctx', 0, 0)  13.6 us
    slice x4, local copies, waits for them, and re-layouts, on_device(): fold_value_rows = value_piece[block_first:block_first + block_size]  10.5 us
  transfers between devices with their start and end apart: 2, of which 1 were waited for; matrix products, arithmetic and copies ran while one was open for 7% of the time, Pallas kernels for 0%

profile of v1, /device:TPU:1, one launch (start us, length us, event | category | flops | bytes accessed | tf_op | source)
XLA Modules:
  0.0 243.6 jit_solution(1093172625096793564)
XLA Ops:
  6.5 3.3 %stack.2 = bf16[16,192,640]{2,1,0:T(8,128)(2,1)} broadcast(bf16[192,640]{1,0:T(8,128)(2,1)} %param.9), dimensions={1,2} | broadcast | bytes 4177920 | tf_op jit(solution)/shard_map/stack | solution.py:89
  9.8 13.6 %all-to-all-start = ((bf16[16,192,640]{2,1,0:T(8,128)(2,1)}), bf16[16,192,640]{2,1,0:T(8,128)(2,1)}, u32[]{:S(2)}, u32[]{:S(2)}) async-start(bf16[16,192,640]{2,1,0:T(8,128)(2,1)} %stack.2), calls=%async_computation | async-start | bytes 7864320 | tf_op jit(solution)/shard_map/all_to_all | solution.py:89
  24.1 15.5 %all-reduce = (f32[192]{0:T(256)S(1)}, f32[192]{0:T(256)S(1)}) all-reduce(f32[192]{0:T(256)S(1)} %fusion.48, f32[192]{0:T(256)S(1)} %fusion.50), channel_id=1, replica_groups=mesh['ctx'=16,'row'=8,'batch'=4] {'row'}, use_global_device_ids=true, to_apply=%region_5.0 | all-reduce | flops 384 | bytes 3072 | tf_op jit(solution)/shard_map/psum | solution.py:62
  39.8 1.0 fusion.83
  41.2 74.6 %psum.21 = s32[4]{0:T(128)S(1)} all-reduce(s32[4]{0:T(128)S(1)} %convert_reduce_fusion.3), channel_id=1, replica_groups=mesh['ctx'=16,'row'=8,'batch'=4] {'ctx'}, use_global_device_ids=true, to_apply=%region_1.0 | all-reduce | flops 4 | bytes 32 | tf_op jit(solution)/shard_map/psum | solution.py:69
  116.0 2.0 pad_maximum_fusion.1
  121.1 1.7 fusion.55
  124.2 3.9 %fusion.81 = (bf16[1024,640]{1,0:T(8,128)(2,1)}, bf16[1024,640]{1,0:T(8,128)(2,1)}, bf16[1024,640]{1,0:T(8,128)(2,1)S(1)}) fusion(bf16[3072,640]{1,0:T(8,128)(2,1)} %bitcast.16), kind=kLoop, calls=%fused_computation.121 | loop fusion | bytes 7864320 | tf_op jit(solution)/shard_map/slice | solution.py:96
  128.2 1.6 copy.67
  129.7 81.2 %all-gather.2.cloned.1.call-done = bf16[3072,640]{1,0:T(8,128)(2,1)} async-done(((bf16[192,640]{1,0:T(8,128)(2,1)}), bf16[3072,640]{1,0:T(8,128)(2,1)}) %all-gather.2.cloned.1.call-update) | async-done | bytes 3932176 | tf_op jit(solution)/shard_map/all_gather | solution.py:87
  211.0 3.5 %fusion.82 = (bf16[1024,640]{1,0:T(8,128)(2,1)S(1)}, bf16[1024,640]{1,0:T(8,128)(2,1)}, bf16[1024,640]{1,0:T(8,128)(2,1)S(1)}) fusion(bf16[3072,640]{1,0:T(8,128)(2,1)} %all-gather.2.cloned.1.call-done), kind=kLoop, calls=%fused_computation.122 | loop fusion | bytes 7864320 | tf_op jit(solution)/shard_map/slice | solution.py:95
  214.5 1.5 copy.90
  216.7 1.6 copy.91
  218.3 2.5 %copy.72 = bf16[1024,640]{0,1:T(8,128)(2,1)} copy(bf16[1024,640]{1,0:T(8,128)(2,1)} %get-tuple-element.18) | data formatting | bytes 2621440 | tf_op jit(solution)/shard_map/slice | solution.py:96
  220.8 2.5 %copy.77 = bf16[1024,640]{0,1:T(8,128)(2,1)} copy(bf16[1024,640]{1,0:T(8,128)(2,1)} %get-tuple-element.17) | data formatting | bytes 2621440 | tf_op jit(solution)/shard_map/slice | solution.py:96
  223.3 2.4 fusion
  225.7 1.1 fusion.2
  226.8 1.1 fusion.1
  227.8 1.3 fusion.7
  229.1 1.3 fusion.5
  230.4 1.3 fusion.3
  231.7 1.3 fusion.39
  233.1 1.3 fusion.33
  234.4 1.3 fusion.45
  (65 shorter events, 7.5 us)
Async XLA Ops:
  9.8 13.7 %copy-start.4 = (bf16[192,640]{1,0:T(8,128)(2,1)S(1)}, bf16[192,640]{1,0:T(8,128)(2,1)}, u32[]{:S(2)}) copy-start(bf16[192,640]{1,0:T(8,128)(2,1)} %param.8) | copy-start | bytes 737284
  9.8 13.9 %copy-start.5 = (bf16[192,640]{1,0:T(8,128)(2,1)S(1)}, bf16[192,640]{1,0:T(8,128)(2,1)}, u32[]{:S(2)}) copy-start(bf16[192,640]{1,0:T(8,128)(2,1)} %param.7) | copy-start | bytes 737284
  9.8 29.8 %copy-start.6 = (f32[640]{0:T(1024)S(1)}, f32[640]{0:T(1024)}, u32[]{:S(2)}) copy-start(f32[640]{0:T(1024)} %param.11) | copy-start | bytes 7684
  9.8 114.4 %all-to-all-start = ((bf16[16,192,640]{2,1,0:T(8,128)(2,1)}), bf16[16,192,640]{2,1,0:T(8,128)(2,1)}, u32[]{:S(2)}, u32[]{:S(2)}) async-start(bf16[16,192,640]{2,1,0:T(8,128)(2,1)} %stack.2), calls=%async_computation | async-start | bytes 7864320 | tf_op jit(solution)/shard_map/all_to_all | solution.py:89
  23.4 17.4 %copy-start.7 = (f32[640]{0:T(1024)S(1)}, f32[640]{0:T(1024)}, u32[]{:S(2)}) copy-start(f32[640]{0:T(1024)} %param.10) | copy-start | bytes 7684
  23.4 187.5 %all-gather.2.cloned.1.call-start = ((), (), s32[]{:S(2)}) async-start(), calls=%async_computation.1 | async-start | bytes 4177920 | tf_op jit(solution)/shard_map/all_gather | solution.py:87
  23.9 17.2 %copy-start.8 = (s32[192]{0:T(256)S(1)}, s32[192]{0:T(256)}, u32[]{:S(2)}) copy-start(s32[192]{0:T(256)} %param.12) | copy-start | bytes 2308
  23.9 92.1 %copy-start.9 = (s32[4,2]{0,1:T(2,128)S(1)}, s32[4,2]{0,1:T(2,128)}, u32[]{:S(2)}) copy-start(s32[4,2]{0,1:T(2,128)} %param.13) | copy-start | bytes 100
  119.0 2.1 copy-start
  229.1 2.6 %copy-start.1 = (bf16[1024,640]{0,1:T(8,128)(2,1)S(1)}, bf16[1024,640]{0,1:T(8,128)(2,1)}, u32[]{:S(2)}) copy-start(bf16[1024,640]{0,1:T(8,128)(2,1)} %copy.67) | copy-start | bytes 3932164
  231.7 1.3 copy-start.3
  233.1 1.3 copy-start.2
Sparse Core Ops, SparseCore 0:
  123.8 87.1 all-gather.1
